TPU v7x, 32 devices: a whole 2x2x4 slice. The times are simulated.
32 devices in a mesh: macro: 8 (over y, x, core), rve: 4 (over z).
Axes of the slice: x: 2, y: 2, z: 4, core: 2. Of those that a mesh axis runs over, the one named last changes fastest.
Arguments:
- deform: float32 [9, 512], P(None, 'macro'), may hold values from -6 to 6
- plastic: int32 [512], P('macro'), may hold values 0 or 1
- route: int32 [512], P('macro'), may hold values from 0 to 7, as said below
- stiff: float32 [8, 1536], P('macro', 'rve'), may hold values from 0.1 to 2
- cubic: float32 [8, 1536], P('macro', 'rve'), may hold values from 0.5 to 5
- coupling: float32 [8, 24, 2, 64, 64], P('macro', 'rve'), may hold values from -0.75 to 0.75
- conn: int32 [8, 24, 2], P('macro', 'rve'), may hold values from 0 to 5
- iface: float32 [8, 256, 64], P('macro', 'rve'), may hold values from -0.75 to 0.75
- load_map: float32 [8, 9, 1536], P('macro', None, 'rve'), may hold values from -2 to 2
- average_map: float32 [8, 9, 1536], P('macro', None, 'rve'), may hold values from -0.15625 to 0.15625
Outputs:
- stress: float32 [9, 512], P(None, 'macro')
- micro_field: float32 [8, 1536, 128], P('macro', 'rve')
Inputs may be any that keep to these rules, and one draw needn't show every extreme that they name: `route`: among the points of one macro section no group is named more than 16 times, and one group is named exactly 16 times by every section. `conn`: an index among the 6 blocks held with the same block row on one device.
All inputs are finite; a program needn't handle non-finite values. No bound on the sum of `plastic` on one device may be relied on, other than what follows from the above.
Results may differ from a plain program's by a relative error of at most 0.0003.
Values sent between devices are 32-bit elements; how exact they have to be, the bound alone decides.
A program may use at most 64 MiB of HBM per device.

v0:
```python
import jax
import jax.numpy as jnp
from jax import lax
from jax.sharding import PartitionSpec as P

ITERS = 2
NEWTON = 2
HIGHEST_PREC = lax.Precision.HIGHEST
EPSILON = 1e-06


def from_behind(block, axis, distance):
    devices = range(lax.axis_size(axis))
    route = [((i - distance) % len(devices), i) for i in devices]
    return lax.ppermute(block, axis, route)


def with_halo(block, sides, width):
    for axis, dim in sides:
        count = lax.axis_size(axis)
        forward = [(i, i + 1) for i in range(count - 1)]
        forward.append((count - 1, 0))
        backward = [(target, source) for source, target in forward]
        low = lax.ppermute(
            lax.slice_in_dim(block, block.shape[dim] - width, None, axis=dim), axis, forward
        )
        high = lax.ppermute(lax.slice_in_dim(block, 0, width, axis=dim), axis, backward)
        block = jnp.concatenate([low, block, high], axis=dim)
    return block


def slot_index(route_rows, capacity):
    point_count = route_rows.shape[0]
    position = jnp.arange(point_count, dtype=jnp.int32)
    same_group = route_rows[:, None] == route_rows[None, :]
    before = position[None, :] < position[:, None]
    rank_in = jnp.sum(
        jnp.where(jnp.logical_and(same_group, before), 1, 0).astype(jnp.int32), axis=1
    )
    return route_rows * capacity + rank_in


def local_matrix(coupling, conn, stiff):
    blocks, slot_count, block_size, _ = coupling.shape
    spring = jnp.einsum("bsxk,bsyk->bsxy", coupling, coupling, precision=HIGHEST_PREC)
    block_ids = jnp.arange(blocks, dtype=jnp.int32)
    own_mark = (block_ids[None, None, :] == block_ids[:, None, None]).astype(jnp.float32)
    far_mark = jnp.logical_and(
        block_ids[None, None, :] == conn[:, :, None], conn[:, :, None] != block_ids[:, None, None]
    ).astype(jnp.float32)
    weight = own_mark - far_mark
    pair_mark = jnp.einsum("bsk,bsl->bskl", weight, weight, precision=HIGHEST_PREC)
    assembled = jnp.einsum("bskl,bsxy->kxly", pair_mark, spring, precision=HIGHEST_PREC)
    assembled = assembled.reshape(blocks * block_size, blocks * block_size)
    return assembled + jnp.diag(stiff)


def norm_sum(values):
    return lax.psum(jnp.sum(values * values, axis=0), "rve")


def split_solve(strain, flag_cols, stiff, cubic, coupling, conn, iface, load_map):
    block_size = coupling.shape[3]
    local_part = local_matrix(coupling[0], conn[0], stiff[0])
    edge_block = iface[0]
    own_spring = jnp.einsum("xk,yk->xy", edge_block, edge_block, precision=HIGHEST_PREC)
    next_edge = from_behind(edge_block, "rve", -1)
    next_spring = jnp.einsum("xk,yk->xy", next_edge, next_edge, precision=HIGHEST_PREC)
    load_cols = jnp.einsum("ci,cp->ip", load_map[0], strain, precision=HIGHEST_PREC)
    hard = flag_cols * cubic[0][:, None]

    def operate(field):
        product = jnp.dot(
            local_part, field, precision=HIGHEST_PREC, preferred_element_type=jnp.float32
        )
        first_rows = field[:block_size]
        last_rows = field[-block_size:]
        end_rows = jnp.concatenate([first_rows, last_rows], axis=0)
        padded = with_halo(end_rows, (("rve", 0),), block_size)
        top_flux = jnp.dot(
            own_spring,
            first_rows - padded[:block_size],
            precision=HIGHEST_PREC,
            preferred_element_type=jnp.float32,
        )
        bottom = jnp.dot(
            next_spring,
            last_rows - padded[-block_size:],
            precision=HIGHEST_PREC,
            preferred_element_type=jnp.float32,
        )
        product = product.at[:block_size].add(top_flux)
        product = product.at[-block_size:].add(bottom)
        return product

    solution = jnp.zeros_like(load_cols)
    for newton_step in range(NEWTON):
        tangent_add = 3.0 * hard * solution * solution
        if newton_step == 0:
            right_side = load_cols
        else:
            right_side = load_cols - operate(solution) - hard * (solution * solution * solution)

        def sweep(turn_index, carried):
            iterate, residue, direct, norm_now = carried
            product = operate(direct) + tangent_add * direct
            curvature_col = lax.psum(jnp.sum(direct * product, axis=0), "rve")
            step_len = norm_now / (curvature_col + EPSILON)
            iterate = iterate + step_len * direct
            residue = residue - step_len * product
            norm_next = norm_sum(residue)
            direct = residue + norm_next / (norm_now + EPSILON) * direct
            return (iterate, residue, direct, norm_next)

        start = (jnp.zeros_like(right_side), right_side, right_side, norm_sum(right_side))
        iterate, residue, direct, norm_now = lax.fori_loop(0, ITERS, sweep, start)
        solution = solution + iterate
    return solution


def shards(deform, plastic, route, stiff, cubic, coupling, conn, iface, load_map, average_map):
    groups = lax.axis_size("macro")
    capacity = 2 * deform.shape[1] // groups
    columns = groups * capacity
    slot_ids = slot_index(route, capacity)
    places = jnp.arange(columns, dtype=jnp.int32)
    select = (slot_ids[:, None] == places[None, :]).astype(jnp.float32)
    outgoing = jnp.dot(
        deform, select, precision=HIGHEST_PREC, preferred_element_type=jnp.float32
    ).reshape(9, groups, capacity)
    flags_out = jnp.dot(
        plastic.astype(jnp.float32)[None, :],
        select,
        precision=HIGHEST_PREC,
        preferred_element_type=jnp.float32,
    ).reshape(1, groups, capacity)
    incoming, flags_in = (
        lax.all_to_all(outgoing, "macro", split_axis=1, concat_axis=1, tiled=True),
        lax.all_to_all(flags_out, "macro", split_axis=1, concat_axis=1, tiled=True),
    )
    strain = incoming.reshape(9, columns)
    flag_cols = flags_in.reshape(1, columns)
    solution = split_solve(strain, flag_cols, stiff, cubic, coupling, conn, iface, load_map)
    part_stress = jnp.einsum("ci,ip->cp", average_map[0], solution, precision=HIGHEST_PREC)
    group_stress = lax.psum(part_stress, "rve")
    returned_rows = lax.all_to_all(
        group_stress.reshape(9, groups, capacity), "macro", split_axis=1, concat_axis=1, tiled=True
    )
    stress = jnp.dot(
        returned_rows.reshape(9, columns),
        select.T,
        precision=HIGHEST_PREC,
        preferred_element_type=jnp.float32,
    )
    return (stress, solution[None])


def solution(mesh):
    return jax.shard_map(
        shards,
        mesh=mesh,
        in_specs=(
            P(None, "macro"),
            P("macro"),
            P("macro"),
            P("macro", "rve"),
            P("macro", "rve"),
            P("macro", "rve", None, None, None),
            P("macro", "rve", None),
            P("macro", "rve", None),
            P("macro", None, "rve"),
            P("macro", None, "rve"),
        ),
        out_specs=(P(None, "macro"), P("macro", "rve", None)),
        check_vma=False,
    )
```

profile of v0, /device:TPU:0, one launch (start us, length us, event | category | flops | bytes accessed | tf_op | source)
XLA Modules:
  0.0 195.9 jit_solution(6440798218701041127)
XLA Ops:
  0.7 0.9 select_reduce_fusion
  1.6 0.7 multiply_add_fusion.4
  2.2 1.7 fusion.23
  3.9 5.2 %all-to-all-start.1 = ((f32[1,8,16]{2,0,1:T(1,128)}), f32[1,8,16]{2,0,1:T(1,128)S(1)}, u32[]{:S(2)}, u32[]{:S(2)}) async-start(f32[1,8,16]{2,0,1:T(1,128)} %fusion.23), calls=%async_computation.1 | async-start | bytes 8192 | tf_op jit(solution)/shard_map/all_to_all | solution.py:139
  9.1 3.6 %collective-permute-start.4 = (f32[64,64]{1,0:T(8,128)}, f32[64,64]{1,0:T(8,128)S(1)}, u32[]{:S(2)}, u32[]{:S(2)}) collective-permute-start(f32[64,64]{1,0:T(8,128)} %bitcast.118), channel_id=1, source_target_pairs={{1,0},{2,1},{3,2},{0,3},{5,4},{6,5},{7,6},{4,7},{9,8},{10,9},{11,1... | collective-permute-start | bytes 49160 | tf_op jit(solution)/shard_map/ppermute | solution.py:15
  12.7 0.7 iota_compare_fusion.7
  13.4 0.7 convert_subtract_fusion
  14.1 0.7 convolution_bitcast_fusion.5
  14.8 1.5 convolution_bitcast_fusion.4
  17.6 0.7 reshape.256
  18.3 4.2 %all-to-all-start = ((f32[8,1,144]{2,1,0:T(1,128)}), f32[8,1,144]{2,1,0:T(1,128)S(1)}, u32[]{:S(2)}, u32[]{:S(2)}) async-start(f32[8,1,144]{2,1,0:T(1,128)} %reshape.256), calls=%async_computation | async-start | bytes 16384 | tf_op jit(solution)/shard_map/all_to_all | solution.py:138
  23.4 0.7 reduce.29
  24.1 3.1 %all-to-all-done = f32[8,1,144]{2,1,0:T(1,128)S(1)} async-done(((f32[8,1,144]{2,1,0:T(1,128)}), f32[8,1,144]{2,1,0:T(1,128)S(1)}, u32[]{:S(2)}, u32[]{:S(2)}) %all-to-all-start) | async-done | bytes 4640 | tf_op jit(solution)/shard_map/all_to_all | solution.py:138
  27.8 0.7 reduce.30
  29.3 8.8 %psum.65 = f32[128]{0:T(128)S(1)} all-reduce(f32[128]{0:T(128)S(1)} %get-tuple-element.577), channel_id=1, replica_groups=mesh['macro'=8,'rve'=4] {'rve'}, use_global_device_ids=true, to_apply=%region_2.3 | all-reduce | flops 128 | bytes 1024 | tf_op jit(solution)/shard_map/psum | solution.py:59
  38.3 54.1 %while.46 = (s32[]{:T(128)}, f32[384,128]{1,0:T(8,128)S(1)}, f32[384,128]{1,0:T(8,128)S(1)}, f32[384,128]{1,0:T(8,128)S(1)}, f32[128]{0:T(128)S(1)}, /*index=5*/...) while((s32[]{:T(128)}, f32[384,128]{1,0:T(8,128)S(1)}, ...), condition=%wide.region_8.9_spmd.clone, body=%wide.region_3.8_spmd.clone.sunk | while | flops 240042496 | bytes 3879119 | solution.py:116
  38.4 1.6 collective-permute-start
  40.0 2.3 %collective-permute-start.1 = (f32[64,128]{1,0:T(8,128)S(1)}, f32[64,128]{1,0:T(8,128)S(1)}, u32[]{:S(2)}, u32[]{:S(2)}) collective-permute-start(f32[64,128]{1,0:T(8,128)S(1)} %get-tuple-element.697), channel_id=1, source_target_pairs={{1,0},{2,1},{3,2},{0,3},{5,4},{6,5},{7,6},{4,7},{9,8},{10,9},{11,1... | collective-permute-start | bytes 98312 | tf_op jit(solution)/shard_map/while/body/eval_jaxpr/ppermute | solution.py:27
  42.9 1.3 collective-permute-done
  44.7 11.9 %psum.76 = f32[128]{0:T(128)S(1)} all-reduce(f32[128]{0:T(128)S(1)} %multiply_reduce_fusion.10), channel_id=1, replica_groups=mesh['macro'=8,'rve'=4] {'rve'}, use_global_device_ids=true, to_apply=%region_5.5 | all-reduce | flops 128 | bytes 1024 | tf_op jit(solution)/shard_map/while/body/eval_jaxpr/psum | solution.py:107
  56.9 8.4 %psum.77 = f32[128]{0:T(128)S(1)} all-reduce(f32[128]{0:T(128)S(1)} %get-tuple-element.700), channel_id=1, replica_groups=mesh['macro'=8,'rve'=4] {'rve'}, use_global_device_ids=true, to_apply=%region_7.7 | all-reduce | flops 128 | bytes 1024 | tf_op jit(solution)/shard_map/while/body/eval_jaxpr/psum | solution.py:59
  65.4 2.0 %collective-permute-start = (f32[64,128]{1,0:T(8,128)S(1)}, f32[64,128]{1,0:T(8,128)S(1)}, u32[]{:S(2)}, u32[]{:S(2)}) collective-permute-start(f32[64,128]{1,0:T(8,128)S(1)} %get-tuple-element.696), channel_id=1, source_target_pairs={{0,1},{1,2},{2,3},{3,0},{4,5},{5,6},{6,7},{7,4},{8,9},{9,10},{10,1... | collective-permute-start | bytes 98312 | tf_op jit(solution)/shard_map/while/body/eval_jaxpr/ppermute | solution.py:24
  67.4 1.9 collective-permute-start.1
  69.9 1.3 collective-permute-done
  71.9 11.8 %psum.76 = f32[128]{0:T(128)S(1)} all-reduce(f32[128]{0:T(128)S(1)} %multiply_reduce_fusion.10), channel_id=1, replica_groups=mesh['macro'=8,'rve'=4] {'rve'}, use_global_device_ids=true, to_apply=%region_5.5 | all-reduce | flops 128 | bytes 1024 | tf_op jit(solution)/shard_map/while/body/eval_jaxpr/psum | solution.py:107
  84.0 8.4 %psum.77 = f32[128]{0:T(128)S(1)} all-reduce(f32[128]{0:T(128)S(1)} %get-tuple-element.700), channel_id=1, replica_groups=mesh['macro'=8,'rve'=4] {'rve'}, use_global_device_ids=true, to_apply=%region_7.7 | all-reduce | flops 128 | bytes 1024 | tf_op jit(solution)/shard_map/while/body/eval_jaxpr/psum | solution.py:59
  92.4 2.0 %collective-permute-start.5 = (f32[64,128]{1,0:T(8,128)S(1)}, f32[64,128]{1,0:T(8,128)S(1)}, u32[]{:S(2)}, u32[]{:S(2)}) collective-permute-start(f32[64,128]{1,0:T(8,128)S(1)} %get-tuple-element.576), channel_id=1, source_target_pairs={{0,1},{1,2},{2,3},{3,0},{4,5},{5,6},{6,7},{7,4},{8,9},{9,10},{10,1... | collective-permute-start | bytes 98312 | tf_op jit(solution)/shard_map/ppermute | solution.py:24
  94.5 0.7 fusion.54
  95.3 1.9 collective-permute-start.6
  97.2 1.0 collective-permute-done.5
  100.7 12.1 %psum.66 = f32[128]{0:T(128)S(1)} all-reduce(f32[128]{0:T(128)S(1)} %get-tuple-element.566), channel_id=1, replica_groups=mesh['macro'=8,'rve'=4] {'rve'}, use_global_device_ids=true, to_apply=%region_10.11 | all-reduce | flops 128 | bytes 1024 | tf_op jit(solution)/shard_map/psum | solution.py:59
  112.8 54.0 %while.47 = (s32[]{:T(128)}, f32[384,128]{1,0:T(8,128)S(1)}, f32[384,128]{1,0:T(8,128)S(1)}, f32[384,128]{1,0:T(8,128)S(1)}, f32[128]{0:T(128)S(1)}, /*index=5*/...) while((s32[]{:T(128)}, f32[384,128]{1,0:T(8,128)S(1)}, ...), condition=%wide.region_16.17_spmd.clone, body=%wide.region_11.16_spmd.clone.sunk | while | flops 239845888 | bytes 4268231 | solution.py:116
  112.9 3.8 %collective-permute-start.3 = (f32[64,128]{1,0:T(8,128)S(1)}, f32[64,128]{1,0:T(8,128)S(1)}, u32[]{:S(2)}, u32[]{:S(2)}) collective-permute-start(f32[64,128]{1,0:T(8,128)S(1)} %get-tuple-element.711), channel_id=1, source_target_pairs={{1,0},{2,1},{3,2},{0,3},{5,4},{6,5},{7,6},{4,7},{9,8},{10,9},{11,1... | collective-permute-start | bytes 98312 | tf_op jit(solution)/shard_map/while/body/eval_jaxpr/ppermute | solution.py:27
  117.3 1.2 collective-permute-done.2
  119.0 12.0 %psum.78 = f32[128]{0:T(128)S(1)} all-reduce(f32[128]{0:T(128)S(1)} %multiply_reduce_fusion.12), channel_id=1, replica_groups=mesh['macro'=8,'rve'=4] {'rve'}, use_global_device_ids=true, to_apply=%region_13.13 | all-reduce | flops 128 | bytes 1024 | tf_op jit(solution)/shard_map/while/body/eval_jaxpr/psum | solution.py:107
  131.2 8.4 %psum.79 = f32[128]{0:T(128)S(1)} all-reduce(f32[128]{0:T(128)S(1)} %get-tuple-element.714), channel_id=1, replica_groups=mesh['macro'=8,'rve'=4] {'rve'}, use_global_device_ids=true, to_apply=%region_15.15 | all-reduce | flops 128 | bytes 1024 | tf_op jit(solution)/shard_map/while/body/eval_jaxpr/psum | solution.py:59
  139.7 2.0 %collective-permute-start.2 = (f32[64,128]{1,0:T(8,128)S(1)}, f32[64,128]{1,0:T(8,128)S(1)}, u32[]{:S(2)}, u32[]{:S(2)}) collective-permute-start(f32[64,128]{1,0:T(8,128)S(1)} %get-tuple-element.710), channel_id=1, source_target_pairs={{0,1},{1,2},{2,3},{3,0},{4,5},{5,6},{6,7},{7,4},{8,9},{9,10},{10,1... | collective-permute-start | bytes 98312 | tf_op jit(solution)/shard_map/while/body/eval_jaxpr/ppermute | solution.py:24
  141.7 1.9 collective-permute-start.3
  144.2 1.3 collective-permute-done.2
  146.3 11.9 %psum.78 = f32[128]{0:T(128)S(1)} all-reduce(f32[128]{0:T(128)S(1)} %multiply_reduce_fusion.12), channel_id=1, replica_groups=mesh['macro'=8,'rve'=4] {'rve'}, use_global_device_ids=true, to_apply=%region_13.13 | all-reduce | flops 128 | bytes 1024 | tf_op jit(solution)/shard_map/while/body/eval_jaxpr/psum | solution.py:107
  158.3 8.4 %psum.79 = f32[128]{0:T(128)S(1)} all-reduce(f32[128]{0:T(128)S(1)} %get-tuple-element.714), channel_id=1, replica_groups=mesh['macro'=8,'rve'=4] {'rve'}, use_global_device_ids=true, to_apply=%region_15.15 | all-reduce | flops 128 | bytes 1024 | tf_op jit(solution)/shard_map/while/body/eval_jaxpr/psum | solution.py:59
  167.2 18.3 %psum.67 = f32[9,8,16]{2,0,1:T(8,128)S(1)} all-reduce(f32[9,8,16]{2,0,1:T(8,128)S(1)} %copy.105), channel_id=1, replica_groups=mesh['macro'=8,'rve'=4] {'rve'}, use_global_device_ids=true, to_apply=%region_17.18 | all-reduce | flops 1152 | bytes 9216 | tf_op jit(solution)/shard_map/psum | solution.py:145
  185.5 0.7 reshape.258
  186.2 3.3 %all-to-all-start.2 = ((f32[8,1,144]{2,1,0:T(1,128)}), f32[8,1,144]{2,1,0:T(1,128)S(1)}, u32[]{:S(2)}, u32[]{:S(2)}) async-start(f32[8,1,144]{2,1,0:T(1,128)} %reshape.258), calls=%async_computation.2 | async-start | bytes 16384 | tf_op jit(solution)/shard_map/all_to_all | solution.py:146
  189.5 0.7 add_bitcast_fusion
  190.2 3.9 %all-to-all-done.2 = f32[8,1,144]{2,1,0:T(1,128)S(1)} async-done(((f32[8,1,144]{2,1,0:T(1,128)}), f32[8,1,144]{2,1,0:T(1,128)S(1)}, u32[]{:S(2)}, u32[]{:S(2)}) %all-to-all-start.2) | async-done | bytes 4640 | tf_op jit(solution)/shard_map/all_to_all | solution.py:146
  194.1 0.7 reduce.31
  195.0 0.8 fusion.31
  (102 shorter events, 12.9 us)
Async XLA Ops:
  0.6 13.4 %copy-start = (f32[1,6,2,64,64]{4,3,2,1,0:T(8,128)S(1)}, f32[1,6,2,64,64]{4,3,2,1,0:T(8,128)}, u32[]{:S(2)}) copy-start(f32[1,6,2,64,64]{4,3,2,1,0:T(8,128)} %param.31) | copy-start | bytes 589828
  3.9 14.4 %all-to-all-start.1 = ((f32[1,8,16]{2,0,1:T(1,128)}), f32[1,8,16]{2,0,1:T(1,128)S(1)}, u32[]{:S(2)}, u32[]{:S(2)}) async-start(f32[1,8,16]{2,0,1:T(1,128)} %fusion.23), calls=%async_computation.1 | async-start | bytes 8192 | tf_op jit(solution)/shard_map/all_to_all | solution.py:139
  9.1 29.1 %collective-permute-start.4 = (f32[64,64]{1,0:T(8,128)}, f32[64,64]{1,0:T(8,128)S(1)}, u32[]{:S(2)}, u32[]{:S(2)}) collective-permute-start(f32[64,64]{1,0:T(8,128)} %bitcast.118), channel_id=1, source_target_pairs={{1,0},{2,1},{3,2},{0,3},{5,4},{6,5},{7,6},{4,7},{9,8},{10,9},{11,1... | collective-permute-start | bytes 49160 | tf_op jit(solution)/shard_map/ppermute | solution.py:15
  16.5 0.7 copy-start.4
  16.5 0.8 copy-start.6
  16.5 6.0 %copy-start.3 = (f32[1,64,64]{2,1,0:T(8,128)S(1)}, f32[1,64,64]{2,1,0:T(8,128)}, u32[]{:S(2)}) copy-start(f32[1,64,64]{2,1,0:T(8,128)} %param.33) | copy-start | bytes 49156
  16.5 6.2 %copy-start.5 = (f32[1,384]{1,0:T(1,128)S(1)}, f32[1,384]{1,0:T(1,128)}, u32[]{:S(2)}) copy-start(f32[1,384]{1,0:T(1,128)} %param.30) | copy-start | bytes 4612
  16.5 12.2 %copy-start.1 = (f32[1,9,384]{2,0,1:T(1,128)S(1)}, f32[1,9,384]{2,0,1:T(1,128)}, u32[]{:S(2)}) copy-start(f32[1,9,384]{2,0,1:T(1,128)} %param.34) | copy-start | bytes 41476
  18.3 8.9 %all-to-all-start = ((f32[8,1,144]{2,1,0:T(1,128)}), f32[8,1,144]{2,1,0:T(1,128)S(1)}, u32[]{:S(2)}, u32[]{:S(2)}) async-start(f32[8,1,144]{2,1,0:T(1,128)} %reshape.256), calls=%async_computation | async-start | bytes 16384 | tf_op jit(solution)/shard_map/all_to_all | solution.py:138
  38.4 5.8 %collective-permute-start = (f32[64,128]{1,0:T(8,128)S(1)}, f32[64,128]{1,0:T(8,128)S(1)}, u32[]{:S(2)}, u32[]{:S(2)}) collective-permute-start(f32[64,128]{1,0:T(8,128)S(1)} %get-tuple-element.696), channel_id=1, source_target_pairs={{0,1},{1,2},{2,3},{3,0},{4,5},{5,6},{6,7},{7,4},{8,9},{9,10},{10,1... | collective-permute-start | bytes 98312 | tf_op jit(solution)/shard_map/while/body/eval_jaxpr/ppermute | solution.py:24
  40.0 4.4 %collective-permute-start.1 = (f32[64,128]{1,0:T(8,128)S(1)}, f32[64,128]{1,0:T(8,128)S(1)}, u32[]{:S(2)}, u32[]{:S(2)}) collective-permute-start(f32[64,128]{1,0:T(8,128)S(1)} %get-tuple-element.697), channel_id=1, source_target_pairs={{1,0},{2,1},{3,2},{0,3},{5,4},{6,5},{7,6},{4,7},{9,8},{10,9},{11,1... | collective-permute-start | bytes 98312 | tf_op jit(solution)/shard_map/while/body/eval_jaxpr/ppermute | solution.py:27
  65.4 5.8 %collective-permute-start = (f32[64,128]{1,0:T(8,128)S(1)}, f32[64,128]{1,0:T(8,128)S(1)}, u32[]{:S(2)}, u32[]{:S(2)}) collective-permute-start(f32[64,128]{1,0:T(8,128)S(1)} %get-tuple-element.696), channel_id=1, source_target_pairs={{0,1},{1,2},{2,3},{3,0},{4,5},{5,6},{6,7},{7,4},{8,9},{9,10},{10,1... | collective-permute-start | bytes 98312 | tf_op jit(solution)/shard_map/while/body/eval_jaxpr/ppermute | solution.py:24
  67.4 4.1 %collective-permute-start.1 = (f32[64,128]{1,0:T(8,128)S(1)}, f32[64,128]{1,0:T(8,128)S(1)}, u32[]{:S(2)}, u32[]{:S(2)}) collective-permute-start(f32[64,128]{1,0:T(8,128)S(1)} %get-tuple-element.697), channel_id=1, source_target_pairs={{1,0},{2,1},{3,2},{0,3},{5,4},{6,5},{7,6},{4,7},{9,8},{10,9},{11,1... | collective-permute-start | bytes 98312 | tf_op jit(solution)/shard_map/while/body/eval_jaxpr/ppermute | solution.py:27
  92.4 5.8 %collective-permute-start.5 = (f32[64,128]{1,0:T(8,128)S(1)}, f32[64,128]{1,0:T(8,128)S(1)}, u32[]{:S(2)}, u32[]{:S(2)}) collective-permute-start(f32[64,128]{1,0:T(8,128)S(1)} %get-tuple-element.576), channel_id=1, source_target_pairs={{0,1},{1,2},{2,3},{3,0},{4,5},{5,6},{6,7},{7,4},{8,9},{9,10},{10,1... | collective-permute-start | bytes 98312 | tf_op jit(solution)/shard_map/ppermute | solution.py:24
  95.3 4.0 %collective-permute-start.6 = (f32[64,128]{1,0:T(8,128)S(1)}, f32[64,128]{1,0:T(8,128)S(1)}, u32[]{:S(2)}, u32[]{:S(2)}) collective-permute-start(f32[64,128]{1,0:T(8,128)S(1)} %get-tuple-element.575), channel_id=1, source_target_pairs={{1,0},{2,1},{3,2},{0,3},{5,4},{6,5},{7,6},{4,7},{9,8},{10,9},{11,1... | collective-permute-start | bytes 98312 | tf_op jit(solution)/shard_map/ppermute | solution.py:27
  112.8 54.0 %copy-start.2 = (f32[1,9,384]{2,0,1:T(1,128)S(1)}, f32[1,9,384]{2,0,1:T(1,128)}, u32[]{:S(2)}) copy-start(f32[1,9,384]{2,0,1:T(1,128)} %param.35) | copy-start | bytes 41476
  112.8 5.8 %collective-permute-start.2 = (f32[64,128]{1,0:T(8,128)S(1)}, f32[64,128]{1,0:T(8,128)S(1)}, u32[]{:S(2)}, u32[]{:S(2)}) collective-permute-start(f32[64,128]{1,0:T(8,128)S(1)} %get-tuple-element.710), channel_id=1, source_target_pairs={{0,1},{1,2},{2,3},{3,0},{4,5},{5,6},{6,7},{7,4},{8,9},{9,10},{10,1... | collective-permute-start | bytes 98312 | tf_op jit(solution)/shard_map/while/body/eval_jaxpr/ppermute | solution.py:24
  112.9 5.9 %collective-permute-start.3 = (f32[64,128]{1,0:T(8,128)S(1)}, f32[64,128]{1,0:T(8,128)S(1)}, u32[]{:S(2)}, u32[]{:S(2)}) collective-permute-start(f32[64,128]{1,0:T(8,128)S(1)} %get-tuple-element.711), channel_id=1, source_target_pairs={{1,0},{2,1},{3,2},{0,3},{5,4},{6,5},{7,6},{4,7},{9,8},{10,9},{11,1... | collective-permute-start | bytes 98312 | tf_op jit(solution)/shard_map/while/body/eval_jaxpr/ppermute | solution.py:27
  139.7 5.8 %collective-permute-start.2 = (f32[64,128]{1,0:T(8,128)S(1)}, f32[64,128]{1,0:T(8,128)S(1)}, u32[]{:S(2)}, u32[]{:S(2)}) collective-permute-start(f32[64,128]{1,0:T(8,128)S(1)} %get-tuple-element.710), channel_id=1, source_target_pairs={{0,1},{1,2},{2,3},{3,0},{4,5},{5,6},{6,7},{7,4},{8,9},{9,10},{10,1... | collective-permute-start | bytes 98312 | tf_op jit(solution)/shard_map/while/body/eval_jaxpr/ppermute | solution.py:24
  141.7 4.3 %collective-permute-start.3 = (f32[64,128]{1,0:T(8,128)S(1)}, f32[64,128]{1,0:T(8,128)S(1)}, u32[]{:S(2)}, u32[]{:S(2)}) collective-permute-start(f32[64,128]{1,0:T(8,128)S(1)} %get-tuple-element.711), channel_id=1, source_target_pairs={{1,0},{2,1},{3,2},{0,3},{5,4},{6,5},{7,6},{4,7},{9,8},{10,9},{11,1... | collective-permute-start | bytes 98312 | tf_op jit(solution)/shard_map/while/body/eval_jaxpr/ppermute | solution.py:27
  186.2 8.0 %all-to-all-start.2 = ((f32[8,1,144]{2,1,0:T(1,128)}), f32[8,1,144]{2,1,0:T(1,128)S(1)}, u32[]{:S(2)}, u32[]{:S(2)}) async-start(f32[8,1,144]{2,1,0:T(1,128)} %reshape.258), calls=%async_computation.2 | async-start | bytes 16384 | tf_op jit(solution)/shard_map/all_to_all | solution.py:146
where the time goes:
time: 197 us; the launch traced here: 196 us
  blocking collectives  120 us (61%)
  starting transfers between devices  35.7 us (18%)
  waiting for transfers between devices  13.8 us (7%)
  matrix products  11.2 us (6%)
  other arithmetic  7.84 us (4%)
  local copies, waits for them, and re-layouts  5.78 us (3%)
    psum x6, blocking collectives, norm_sum(): return lax.psum(jnp.sum(values * values, axis=0), 'rve')  54.4 us
    psum x4, blocking collectives, sweep(): curvature_col = lax.psum(jnp.sum(direct * product, axis=0), 'rve')  47.6 us
    psum x1, blocking collectives, shards(): group_stress = lax.psum(part_stress, 'rve')  18.3 us
    ppermute x5, starting transfers between devices, with_halo(): lax.ppermute(lax.slice_in_dim(block, 0, width, axis=dim), axis, backward)  11.7 us
    ppermute x5, starting transfers between devices, with_halo(): lax.ppermute(lax.slice_in_dim(block, block.shape[dim] - width, None, axis...  7.7 us
    ppermute x5, waiting for transfers between devices, with_halo(): lax.ppermute(lax.slice_in_dim(block, block.shape[dim] - width, None, axis...  6.12 us
    all_to_all x1, starting transfers between devices, shards(): lax.all_to_all(flags_out, 'macro', split_axis=1, concat_axis=1, tiled=True)  5.17 us
    all_to_all x1, starting transfers between devices, shards(): lax.all_to_all(outgoing, 'macro', split_axis=1, concat_axis=1, tiled=True)  4.2 us
  transfers between devices with their start and end apart: 14, of which 10 were waited for; matrix products, arithmetic and copies ran while one was open for 7% of the time, Pallas kernels for 0%

commit v1 on v0

--- a/solution.py
+++ b/solution.py
@@ -1,3 +1,4 @@
+import functools
 import jax
 import jax.numpy as jnp
 from jax import lax
@@ -7,6 +8,16 @@
 NEWTON = 2
 HIGHEST_PREC = lax.Precision.HIGHEST
 EPSILON = 1e-06
+
+
+def step_on_quotas_now(chunk, link_axis, dim_at, dim_k):
+    outer = jnp.split(chunk, lax.axis_size(link_axis), dim_at)
+    fresh = jnp.stack(outer)
+    then = lax.all_to_all(fresh, link_axis, 0, 0)
+    return jnp.concatenate(then, dim_k)
+
+
+refer_leaves = functools.partial(step_on_quotas_now, link_axis="macro", dim_at=1, dim_k=1)
 
 
 def from_behind(block, axis, distance):
@@ -136,7 +147,7 @@
     ).reshape(1, groups, capacity)
     incoming, flags_in = (
         lax.all_to_all(outgoing, "macro", split_axis=1, concat_axis=1, tiled=True),
-        lax.all_to_all(flags_out, "macro", split_axis=1, concat_axis=1, tiled=True),
+        refer_leaves(flags_out),
     )
     strain = incoming.reshape(9, columns)
     flag_cols = flags_in.reshape(1, columns)

time: 197 us -> 200 us (1.015)
  local copies, waits for them, and re-layouts: 5.78 us -> 9.98 us
    unnamed x23 -> x30, local copies, waits for them, and re-layouts: 2.24 us -> 5.85 us
where the time goes in v1:
time: 200 us; the launch traced here: 199 us
  blocking collectives  120 us (60%)
  starting transfers between devices  35.7 us (18%)
  waiting for transfers between devices  13.8 us (7%)
  matrix products  10.4 us (5%)
  local copies, waits for them, and re-layouts  9.98 us (5%)
  other arithmetic  7.84 us (4%)
    psum x6, blocking collectives, norm_sum(): return lax.psum(jnp.sum(values * values, axis=0), 'rve')  54.4 us
    psum x4, blocking collectives, sweep(): curvature_col = lax.psum(jnp.sum(direct * product, axis=0), 'rve')  47.6 us
    psum x1, blocking collectives, shards(): group_stress = lax.psum(part_stress, 'rve')  18.3 us
    ppermute x5, starting transfers between devices, with_halo(): lax.ppermute(lax.slice_in_dim(block, 0, width, axis=dim), axis, backward)  11.7 us
    ppermute x5, starting transfers between devices, with_halo(): lax.ppermute(lax.slice_in_dim(block, block.shape[dim] - width, None, axis...  7.7 us
    ppermute x5, waiting for transfers between devices, with_halo(): lax.ppermute(lax.slice_in_dim(block, block.shape[dim] - width, None, axis...  6.12 us
    unnamed x30, local copies, waits for them, and re-layouts  5.85 us
    all_to_all x1, starting transfers between devices, step_on_quotas_now(): then = lax.all_to_all(fresh, link_axis, 0, 0)  5.17 us
  transfers between devices with their start and end apart: 14, of which 10 were waited for; matrix products, arithmetic and copies ran while one was open for 7% of the time, Pallas kernels for 0%

profile of v1, /device:TPU:0, one launch (start us, length us, event | category | flops | bytes accessed | tf_op | source)
XLA Modules:
  0.0 199.2 jit_solution(13101435723796853879)
XLA Ops:
  0.6 0.9 select_reduce_fusion
  1.6 0.7 multiply_add_fusion.3
  2.2 0.8 convolution_bitcast_fusion.9
  7.3 5.2 %all-to-all-start.1 = ((f32[8,1,1,16]{3,2,1,0:T(1,128)}), f32[8,1,1,16]{3,2,1,0:T(1,128)S(1)}, u32[]{:S(2)}, u32[]{:S(2)}) async-start(f32[8,1,1,16]{3,2,1,0:T(1,128)} %constant_dynamic-update-slice_fusion), calls=%async_computation.1 | async-start | bytes 8192 | tf_op jit(solution)/shard_map/all_to_all | solution.py:16
  12.4 3.6 %collective-permute-start.4 = (f32[64,64]{1,0:T(8,128)}, f32[64,64]{1,0:T(8,128)S(1)}, u32[]{:S(2)}, u32[]{:S(2)}) collective-permute-start(f32[64,64]{1,0:T(8,128)} %bitcast.130), channel_id=1, source_target_pairs={{1,0},{2,1},{3,2},{0,3},{5,4},{6,5},{7,6},{4,7},{9,8},{10,9},{11,1... | collective-permute-start | bytes 49160 | tf_op jit(solution)/shard_map/ppermute | solution.py:26
  16.1 0.7 iota_compare_fusion.8
  16.7 0.7 convert_subtract_fusion
  17.4 0.7 convolution_bitcast_fusion.5
  18.2 1.5 convolution_bitcast_fusion.4
  21.0 0.7 reshape.241
  21.7 4.2 %all-to-all-start = ((f32[8,1,144]{2,1,0:T(1,128)}), f32[8,1,144]{2,1,0:T(1,128)S(1)}, u32[]{:S(2)}, u32[]{:S(2)}) async-start(f32[8,1,144]{2,1,0:T(1,128)} %reshape.241), calls=%async_computation | async-start | bytes 16384 | tf_op jit(solution)/shard_map/all_to_all | solution.py:149
  26.7 0.7 reduce.29
  27.5 3.1 %all-to-all-done = f32[8,1,144]{2,1,0:T(1,128)S(1)} async-done(((f32[8,1,144]{2,1,0:T(1,128)}), f32[8,1,144]{2,1,0:T(1,128)S(1)}, u32[]{:S(2)}, u32[]{:S(2)}) %all-to-all-start) | async-done | bytes 4640 | tf_op jit(solution)/shard_map/all_to_all | solution.py:149
  31.2 0.7 reduce.30
  32.7 8.8 %psum.65 = f32[128]{0:T(128)S(1)} all-reduce(f32[128]{0:T(128)S(1)} %get-tuple-element.577), channel_id=1, replica_groups=mesh['macro'=8,'rve'=4] {'rve'}, use_global_device_ids=true, to_apply=%region_2.3 | all-reduce | flops 128 | bytes 1024 | tf_op jit(solution)/shard_map/psum | solution.py:70
  41.7 54.1 %while.46 = (s32[]{:T(128)}, f32[384,128]{1,0:T(8,128)S(1)}, f32[384,128]{1,0:T(8,128)S(1)}, f32[384,128]{1,0:T(8,128)S(1)}, f32[128]{0:T(128)S(1)}, /*index=5*/...) while((s32[]{:T(128)}, f32[384,128]{1,0:T(8,128)S(1)}, ...), condition=%wide.region_8.9_spmd.clone, body=%wide.region_3.8_spmd.clone.sunk | while | flops 240042496 | bytes 3879119 | solution.py:127
  41.8 1.6 collective-permute-start
  43.3 2.3 %collective-permute-start.1 = (f32[64,128]{1,0:T(8,128)S(1)}, f32[64,128]{1,0:T(8,128)S(1)}, u32[]{:S(2)}, u32[]{:S(2)}) collective-permute-start(f32[64,128]{1,0:T(8,128)S(1)} %get-tuple-element.697), channel_id=1, source_target_pairs={{1,0},{2,1},{3,2},{0,3},{5,4},{6,5},{7,6},{4,7},{9,8},{10,9},{11,1... | collective-permute-start | bytes 98312 | tf_op jit(solution)/shard_map/while/body/eval_jaxpr/ppermute | solution.py:38
  46.3 1.3 collective-permute-done
  48.1 11.9 %psum.76 = f32[128]{0:T(128)S(1)} all-reduce(f32[128]{0:T(128)S(1)} %multiply_reduce_fusion.10), channel_id=1, replica_groups=mesh['macro'=8,'rve'=4] {'rve'}, use_global_device_ids=true, to_apply=%region_5.5 | all-reduce | flops 128 | bytes 1024 | tf_op jit(solution)/shard_map/while/body/eval_jaxpr/psum | solution.py:118
  60.3 8.4 %psum.77 = f32[128]{0:T(128)S(1)} all-reduce(f32[128]{0:T(128)S(1)} %get-tuple-element.700), channel_id=1, replica_groups=mesh['macro'=8,'rve'=4] {'rve'}, use_global_device_ids=true, to_apply=%region_7.7 | all-reduce | flops 128 | bytes 1024 | tf_op jit(solution)/shard_map/while/body/eval_jaxpr/psum | solution.py:70
  68.8 2.0 %collective-permute-start = (f32[64,128]{1,0:T(8,128)S(1)}, f32[64,128]{1,0:T(8,128)S(1)}, u32[]{:S(2)}, u32[]{:S(2)}) collective-permute-start(f32[64,128]{1,0:T(8,128)S(1)} %get-tuple-element.696), channel_id=1, source_target_pairs={{0,1},{1,2},{2,3},{3,0},{4,5},{5,6},{6,7},{7,4},{8,9},{9,10},{10,1... | collective-permute-start | bytes 98312 | tf_op jit(solution)/shard_map/while/body/eval_jaxpr/ppermute | solution.py:35
  70.8 1.9 collective-permute-start.1
  73.3 1.3 collective-permute-done
  75.2 11.8 %psum.76 = f32[128]{0:T(128)S(1)} all-reduce(f32[128]{0:T(128)S(1)} %multiply_reduce_fusion.10), channel_id=1, replica_groups=mesh['macro'=8,'rve'=4] {'rve'}, use_global_device_ids=true, to_apply=%region_5.5 | all-reduce | flops 128 | bytes 1024 | tf_op jit(solution)/shard_map/while/body/eval_jaxpr/psum | solution.py:118
  87.3 8.4 %psum.77 = f32[128]{0:T(128)S(1)} all-reduce(f32[128]{0:T(128)S(1)} %get-tuple-element.700), channel_id=1, replica_groups=mesh['macro'=8,'rve'=4] {'rve'}, use_global_device_ids=true, to_apply=%region_7.7 | all-reduce | flops 128 | bytes 1024 | tf_op jit(solution)/shard_map/while/body/eval_jaxpr/psum | solution.py:70
  95.8 2.0 %collective-permute-start.5 = (f32[64,128]{1,0:T(8,128)S(1)}, f32[64,128]{1,0:T(8,128)S(1)}, u32[]{:S(2)}, u32[]{:S(2)}) collective-permute-start(f32[64,128]{1,0:T(8,128)S(1)} %get-tuple-element.576), channel_id=1, source_target_pairs={{0,1},{1,2},{2,3},{3,0},{4,5},{5,6},{6,7},{7,4},{8,9},{9,10},{10,1... | collective-permute-start | bytes 98312 | tf_op jit(solution)/shard_map/ppermute | solution.py:35
  97.8 0.7 fusion.51
  98.7 1.9 collective-permute-start.6
  100.6 1.0 collective-permute-done.5
  104.1 12.1 %psum.66 = f32[128]{0:T(128)S(1)} all-reduce(f32[128]{0:T(128)S(1)} %get-tuple-element.566), channel_id=1, replica_groups=mesh['macro'=8,'rve'=4] {'rve'}, use_global_device_ids=true, to_apply=%region_10.11 | all-reduce | flops 128 | bytes 1024 | tf_op jit(solution)/shard_map/psum | solution.py:70
  116.2 54.0 %while.47 = (s32[]{:T(128)}, f32[384,128]{1,0:T(8,128)S(1)}, f32[384,128]{1,0:T(8,128)S(1)}, f32[384,128]{1,0:T(8,128)S(1)}, f32[128]{0:T(128)S(1)}, /*index=5*/...) while((s32[]{:T(128)}, f32[384,128]{1,0:T(8,128)S(1)}, ...), condition=%wide.region_16.17_spmd.clone, body=%wide.region_11.16_spmd.clone.sunk | while | flops 239845888 | bytes 4268231 | solution.py:127
  116.3 3.8 %collective-permute-start.3 = (f32[64,128]{1,0:T(8,128)S(1)}, f32[64,128]{1,0:T(8,128)S(1)}, u32[]{:S(2)}, u32[]{:S(2)}) collective-permute-start(f32[64,128]{1,0:T(8,128)S(1)} %get-tuple-element.711), channel_id=1, source_target_pairs={{1,0},{2,1},{3,2},{0,3},{5,4},{6,5},{7,6},{4,7},{9,8},{10,9},{11,1... | collective-permute-start | bytes 98312 | tf_op jit(solution)/shard_map/while/body/eval_jaxpr/ppermute | solution.py:38
  120.7 1.2 collective-permute-done.2
  122.4 12.0 %psum.78 = f32[128]{0:T(128)S(1)} all-reduce(f32[128]{0:T(128)S(1)} %multiply_reduce_fusion.12), channel_id=1, replica_groups=mesh['macro'=8,'rve'=4] {'rve'}, use_global_device_ids=true, to_apply=%region_13.13 | all-reduce | flops 128 | bytes 1024 | tf_op jit(solution)/shard_map/while/body/eval_jaxpr/psum | solution.py:118
  134.6 8.4 %psum.79 = f32[128]{0:T(128)S(1)} all-reduce(f32[128]{0:T(128)S(1)} %get-tuple-element.714), channel_id=1, replica_groups=mesh['macro'=8,'rve'=4] {'rve'}, use_global_device_ids=true, to_apply=%region_15.15 | all-reduce | flops 128 | bytes 1024 | tf_op jit(solution)/shard_map/while/body/eval_jaxpr/psum | solution.py:70
  143.1 2.0 %collective-permute-start.2 = (f32[64,128]{1,0:T(8,128)S(1)}, f32[64,128]{1,0:T(8,128)S(1)}, u32[]{:S(2)}, u32[]{:S(2)}) collective-permute-start(f32[64,128]{1,0:T(8,128)S(1)} %get-tuple-element.710), channel_id=1, source_target_pairs={{0,1},{1,2},{2,3},{3,0},{4,5},{5,6},{6,7},{7,4},{8,9},{9,10},{10,1... | collective-permute-start | bytes 98312 | tf_op jit(solution)/shard_map/while/body/eval_jaxpr/ppermute | solution.py:35
  145.1 1.9 collective-permute-start.3
  147.6 1.3 collective-permute-done.2
  149.6 11.9 %psum.78 = f32[128]{0:T(128)S(1)} all-reduce(f32[128]{0:T(128)S(1)} %multiply_reduce_fusion.12), channel_id=1, replica_groups=mesh['macro'=8,'rve'=4] {'rve'}, use_global_device_ids=true, to_apply=%region_13.13 | all-reduce | flops 128 | bytes 1024 | tf_op jit(solution)/shard_map/while/body/eval_jaxpr/psum | solution.py:118
  161.7 8.4 %psum.79 = f32[128]{0:T(128)S(1)} all-reduce(f32[128]{0:T(128)S(1)} %get-tuple-element.714), channel_id=1, replica_groups=mesh['macro'=8,'rve'=4] {'rve'}, use_global_device_ids=true, to_apply=%region_15.15 | all-reduce | flops 128 | bytes 1024 | tf_op jit(solution)/shard_map/while/body/eval_jaxpr/psum | solution.py:70
  170.6 18.3 %psum.67 = f32[9,8,16]{2,0,1:T(8,128)S(1)} all-reduce(f32[9,8,16]{2,0,1:T(8,128)S(1)} %copy.102), channel_id=1, replica_groups=mesh['macro'=8,'rve'=4] {'rve'}, use_global_device_ids=true, to_apply=%region_17.18 | all-reduce | flops 1152 | bytes 9216 | tf_op jit(solution)/shard_map/psum | solution.py:156
  188.9 0.7 reshape.243
  189.5 3.3 %all-to-all-start.2 = ((f32[8,1,144]{2,1,0:T(1,128)}), f32[8,1,144]{2,1,0:T(1,128)S(1)}, u32[]{:S(2)}, u32[]{:S(2)}) async-start(f32[8,1,144]{2,1,0:T(1,128)} %reshape.243), calls=%async_computation.2 | async-start | bytes 16384 | tf_op jit(solution)/shard_map/all_to_all | solution.py:157
  192.9 0.7 add_bitcast_fusion
  193.6 3.9 %all-to-all-done.2 = f32[8,1,144]{2,1,0:T(1,128)S(1)} async-done(((f32[8,1,144]{2,1,0:T(1,128)}), f32[8,1,144]{2,1,0:T(1,128)S(1)}, u32[]{:S(2)}, u32[]{:S(2)}) %all-to-all-start.2) | async-done | bytes 4640 | tf_op jit(solution)/shard_map/all_to_all | solution.py:157
  197.5 0.7 reduce.31
  198.4 0.8 fusion.27
  (110 shorter events, 17.1 us)
Async XLA Ops:
  0.6 16.8 %copy-start = (f32[1,6,2,64,64]{4,3,2,1,0:T(8,128)S(1)}, f32[1,6,2,64,64]{4,3,2,1,0:T(8,128)}, u32[]{:S(2)}) copy-start(f32[1,6,2,64,64]{4,3,2,1,0:T(8,128)} %param.31) | copy-start | bytes 589828
  7.3 14.4 %all-to-all-start.1 = ((f32[8,1,1,16]{3,2,1,0:T(1,128)}), f32[8,1,1,16]{3,2,1,0:T(1,128)S(1)}, u32[]{:S(2)}, u32[]{:S(2)}) async-start(f32[8,1,1,16]{3,2,1,0:T(1,128)} %constant_dynamic-update-slice_fusion), calls=%async_computation.1 | async-start | bytes 8192 | tf_op jit(solution)/shard_map/all_to_all | solution.py:16
  12.4 29.1 %collective-permute-start.4 = (f32[64,64]{1,0:T(8,128)}, f32[64,64]{1,0:T(8,128)S(1)}, u32[]{:S(2)}, u32[]{:S(2)}) collective-permute-start(f32[64,64]{1,0:T(8,128)} %bitcast.130), channel_id=1, source_target_pairs={{1,0},{2,1},{3,2},{0,3},{5,4},{6,5},{7,6},{4,7},{9,8},{10,9},{11,1... | collective-permute-start | bytes 49160 | tf_op jit(solution)/shard_map/ppermute | solution.py:26
  19.8 0.7 copy-start.4
  19.9 0.8 copy-start.6
  19.9 6.0 %copy-start.3 = (f32[1,64,64]{2,1,0:T(8,128)S(1)}, f32[1,64,64]{2,1,0:T(8,128)}, u32[]{:S(2)}) copy-start(f32[1,64,64]{2,1,0:T(8,128)} %param.33) | copy-start | bytes 49156
  19.9 6.2 %copy-start.5 = (f32[1,384]{1,0:T(1,128)S(1)}, f32[1,384]{1,0:T(1,128)}, u32[]{:S(2)}) copy-start(f32[1,384]{1,0:T(1,128)} %param.30) | copy-start | bytes 4612
  19.9 12.2 %copy-start.1 = (f32[1,9,384]{2,0,1:T(1,128)S(1)}, f32[1,9,384]{2,0,1:T(1,128)}, u32[]{:S(2)}) copy-start(f32[1,9,384]{2,0,1:T(1,128)} %param.34) | copy-start | bytes 41476
  21.7 8.9 %all-to-all-start = ((f32[8,1,144]{2,1,0:T(1,128)}), f32[8,1,144]{2,1,0:T(1,128)S(1)}, u32[]{:S(2)}, u32[]{:S(2)}) async-start(f32[8,1,144]{2,1,0:T(1,128)} %reshape.241), calls=%async_computation | async-start | bytes 16384 | tf_op jit(solution)/shard_map/all_to_all | solution.py:149
  41.8 5.8 %collective-permute-start = (f32[64,128]{1,0:T(8,128)S(1)}, f32[64,128]{1,0:T(8,128)S(1)}, u32[]{:S(2)}, u32[]{:S(2)}) collective-permute-start(f32[64,128]{1,0:T(8,128)S(1)} %get-tuple-element.696), channel_id=1, source_target_pairs={{0,1},{1,2},{2,3},{3,0},{4,5},{5,6},{6,7},{7,4},{8,9},{9,10},{10,1... | collective-permute-start | bytes 98312 | tf_op jit(solution)/shard_map/while/body/eval_jaxpr/ppermute | solution.py:35
  43.3 4.4 %collective-permute-start.1 = (f32[64,128]{1,0:T(8,128)S(1)}, f32[64,128]{1,0:T(8,128)S(1)}, u32[]{:S(2)}, u32[]{:S(2)}) collective-permute-start(f32[64,128]{1,0:T(8,128)S(1)} %get-tuple-element.697), channel_id=1, source_target_pairs={{1,0},{2,1},{3,2},{0,3},{5,4},{6,5},{7,6},{4,7},{9,8},{10,9},{11,1... | collective-permute-start | bytes 98312 | tf_op jit(solution)/shard_map/while/body/eval_jaxpr/ppermute | solution.py:38
  68.8 5.8 %collective-permute-start = (f32[64,128]{1,0:T(8,128)S(1)}, f32[64,128]{1,0:T(8,128)S(1)}, u32[]{:S(2)}, u32[]{:S(2)}) collective-permute-start(f32[64,128]{1,0:T(8,128)S(1)} %get-tuple-element.696), channel_id=1, source_target_pairs={{0,1},{1,2},{2,3},{3,0},{4,5},{5,6},{6,7},{7,4},{8,9},{9,10},{10,1... | collective-permute-start | bytes 98312 | tf_op jit(solution)/shard_map/while/body/eval_jaxpr/ppermute | solution.py:35
  70.8 4.1 %collective-permute-start.1 = (f32[64,128]{1,0:T(8,128)S(1)}, f32[64,128]{1,0:T(8,128)S(1)}, u32[]{:S(2)}, u32[]{:S(2)}) collective-permute-start(f32[64,128]{1,0:T(8,128)S(1)} %get-tuple-element.697), channel_id=1, source_target_pairs={{1,0},{2,1},{3,2},{0,3},{5,4},{6,5},{7,6},{4,7},{9,8},{10,9},{11,1... | collective-permute-start | bytes 98312 | tf_op jit(solution)/shard_map/while/body/eval_jaxpr/ppermute | solution.py:38
  95.8 5.8 %collective-permute-start.5 = (f32[64,128]{1,0:T(8,128)S(1)}, f32[64,128]{1,0:T(8,128)S(1)}, u32[]{:S(2)}, u32[]{:S(2)}) collective-permute-start(f32[64,128]{1,0:T(8,128)S(1)} %get-tuple-element.576), channel_id=1, source_target_pairs={{0,1},{1,2},{2,3},{3,0},{4,5},{5,6},{6,7},{7,4},{8,9},{9,10},{10,1... | collective-permute-start | bytes 98312 | tf_op jit(solution)/shard_map/ppermute | solution.py:35
  98.7 4.0 %collective-permute-start.6 = (f32[64,128]{1,0:T(8,128)S(1)}, f32[64,128]{1,0:T(8,128)S(1)}, u32[]{:S(2)}, u32[]{:S(2)}) collective-permute-start(f32[64,128]{1,0:T(8,128)S(1)} %get-tuple-element.575), channel_id=1, source_target_pairs={{1,0},{2,1},{3,2},{0,3},{5,4},{6,5},{7,6},{4,7},{9,8},{10,9},{11,1... | collective-permute-start | bytes 98312 | tf_op jit(solution)/shard_map/ppermute | solution.py:38
  116.2 54.0 %copy-start.2 = (f32[1,9,384]{2,0,1:T(1,128)S(1)}, f32[1,9,384]{2,0,1:T(1,128)}, u32[]{:S(2)}) copy-start(f32[1,9,384]{2,0,1:T(1,128)} %param.35) | copy-start | bytes 41476
  116.2 5.8 %collective-permute-start.2 = (f32[64,128]{1,0:T(8,128)S(1)}, f32[64,128]{1,0:T(8,128)S(1)}, u32[]{:S(2)}, u32[]{:S(2)}) collective-permute-start(f32[64,128]{1,0:T(8,128)S(1)} %get-tuple-element.710), channel_id=1, source_target_pairs={{0,1},{1,2},{2,3},{3,0},{4,5},{5,6},{6,7},{7,4},{8,9},{9,10},{10,1... | collective-permute-start | bytes 98312 | tf_op jit(solution)/shard_map/while/body/eval_jaxpr/ppermute | solution.py:35
  116.3 5.9 %collective-permute-start.3 = (f32[64,128]{1,0:T(8,128)S(1)}, f32[64,128]{1,0:T(8,128)S(1)}, u32[]{:S(2)}, u32[]{:S(2)}) collective-permute-start(f32[64,128]{1,0:T(8,128)S(1)} %get-tuple-element.711), channel_id=1, source_target_pairs={{1,0},{2,1},{3,2},{0,3},{5,4},{6,5},{7,6},{4,7},{9,8},{10,9},{11,1... | collective-permute-start | bytes 98312 | tf_op jit(solution)/shard_map/while/body/eval_jaxpr/ppermute | solution.py:38
  143.1 5.8 %collective-permute-start.2 = (f32[64,128]{1,0:T(8,128)S(1)}, f32[64,128]{1,0:T(8,128)S(1)}, u32[]{:S(2)}, u32[]{:S(2)}) collective-permute-start(f32[64,128]{1,0:T(8,128)S(1)} %get-tuple-element.710), channel_id=1, source_target_pairs={{0,1},{1,2},{2,3},{3,0},{4,5},{5,6},{6,7},{7,4},{8,9},{9,10},{10,1... | collective-permute-start | bytes 98312 | tf_op jit(solution)/shard_map/while/body/eval_jaxpr/ppermute | solution.py:35
  145.1 4.3 %collective-permute-start.3 = (f32[64,128]{1,0:T(8,128)S(1)}, f32[64,128]{1,0:T(8,128)S(1)}, u32[]{:S(2)}, u32[]{:S(2)}) collective-permute-start(f32[64,128]{1,0:T(8,128)S(1)} %get-tuple-element.711), channel_id=1, source_target_pairs={{1,0},{2,1},{3,2},{0,3},{5,4},{6,5},{7,6},{4,7},{9,8},{10,9},{11,1... | collective-permute-start | bytes 98312 | tf_op jit(solution)/shard_map/while/body/eval_jaxpr/ppermute | solution.py:38
  189.5 8.0 %all-to-all-start.2 = ((f32[8,1,144]{2,1,0:T(1,128)}), f32[8,1,144]{2,1,0:T(1,128)S(1)}, u32[]{:S(2)}, u32[]{:S(2)}) async-start(f32[8,1,144]{2,1,0:T(1,128)} %reshape.243), calls=%async_computation.2 | async-start | bytes 16384 | tf_op jit(solution)/shard_map/all_to_all | solution.py:157
